TPU v7x, 32 devices: a whole 2x2x4 slice. The times are simulated.
32 devices in a mesh: space: 16 (over z, x, core), chan: 2 (over y).
Axes of the slice: x: 2, y: 2, z: 4, core: 2. Of those that a mesh axis runs over, the one named last changes fastest.
Arguments:
- state: bfloat16 [96, 512, 1024], P('space', 'chan'), may hold values from -6 to 6
- cotangent: bfloat16 [96, 512, 1024], P('space', None, 'chan'), may hold values from -6 to 6
- order_table: int32 [96], replicated, may hold values from 0 to 95, as said below
- quad_weight: float32 [96], P('space'), may hold values from 0.5 to 2
- legendre: bfloat16 [96, 96, 96], P('space', 'chan'), as said below
- spec_gain: float32 [96, 512], P('chan'), may hold values from 0.5 to 2
- spectral_weight: bfloat16 [2, 512, 512], replicated, may hold values from -0.1875 to 0.1875
- mlp_in: bfloat16 [512, 768], P('chan'), may hold values from -0.25 to 0.25
- mlp_out: bfloat16 [768, 512], P('chan'), may hold values from -0.21875 to 0.21875
Outputs:
- output: bfloat16 [96, 512, 1024], P('space', None, 'chan')
- state_grad: bfloat16 [96, 512, 1024], P('space', 'chan')
Inputs may be any that keep to these rules, and one draw needn't show every extreme that they name: order_table holds each of 0 to 95 once; slots 2 j and 2 j + 1 hold orders m and 95 - m with m < 48. legendre[k, l, t] is zero for every degree l below order_table[k].
All inputs are finite; a program needn't handle non-finite values.
Results may differ from a plain program's by a relative error of at most 0.015.
Values may be sent and summed in bfloat16 or wider, within the bound.
A program may use at most 64 MiB of HBM per device.

v0:
```python
import functools
import math

import jax
import jax.numpy as jnp
from jax import lax
from jax.experimental import pallas as pl
from jax.experimental.pallas import tpu as pltpu
from jax.sharding import PartitionSpec as P

BF = jnp.bfloat16
F32 = jnp.float32
BOTH = ("space", "chan")
ROOT = math.sqrt(2.0 / math.pi)


def transform_table(order_table, lon_count):
    points = lax.broadcasted_iota(jnp.int32, (lon_count, 2 * order_table.shape[0]), 0)
    column = lax.broadcasted_iota(jnp.int32, (lon_count, 2 * order_table.shape[0]), 1)
    phases = points * jnp.repeat(order_table, 2)[None, :] % lon_count
    angles = phases.astype(F32) * (2.0 * math.pi / lon_count)
    waves = jnp.where(column % 2 == 0, jnp.cos(angles), -jnp.sin(angles))
    return (waves * (1.0 / math.sqrt(lon_count))).astype(BF)


def chan_swap(values, split_axis, concat_axis):
    count = lax.axis_size("chan")
    me = lax.axis_index("chan")
    width = values.shape[split_axis] // count
    depth = values.shape[concat_axis]
    shape = list(values.shape)
    shape[split_axis] = width
    shape[concat_axis] = depth * count
    result = jnp.zeros(shape, values.dtype)
    for shift in range(count):
        piece = lax.dynamic_slice_in_dim(values, (me + shift) % count * width, width, split_axis)
        if shift:
            ring = [(i, (i + shift) % count) for i in range(count)]
            piece = lax.ppermute(piece, "chan", ring)
        source = (me - shift + count) % count
        result = lax.dynamic_update_slice_in_dim(result, piece, source * depth, concat_axis)
    return result


def chan_rows(values, share):
    count = lax.axis_size("chan")
    me = lax.axis_index("chan")
    rows = values.shape[0]
    result = jnp.zeros((rows * count,) + values.shape[1:], values.dtype)
    result = lax.dynamic_update_slice_in_dim(result, values, me * rows, 0)
    space = lax.axis_size("space")
    share = share and space % 2 == 0
    parity = lax.axis_index("space") % 2
    part = rows // 2 if share else rows
    mine = lax.dynamic_slice_in_dim(values, parity * part, part, 0) if share else values
    for shift in range(1, count):
        ring = [(i, (i + shift) % count) for i in range(count)]
        source = (me - shift + count) % count
        piece = lax.ppermute(mine, "chan", ring)
        if share:
            other = lax.ppermute(piece, "space", [(i, i ^ 1) for i in range(space)])
            result = lax.dynamic_update_slice_in_dim(
                result, piece, source * rows + parity * part, 0
            )
            result = lax.dynamic_update_slice_in_dim(
                result, other, source * rows + (1 - parity) * part, 0
            )
        else:
            result = lax.dynamic_update_slice_in_dim(result, piece, source * rows, 0)
    return result


def dot(left, right, dims):
    return lax.dot_general(left, right, (dims, ((), ())), preferred_element_type=F32)


def mlp_kernel(state, cot, synth, table, first, first_t, second, second_t, out, grad, spec):
    grid_table = table[...]
    wave = dot(synth[0], grid_table, ((0,), (0,)))
    hidden = (state[0].astype(F32) + wave).astype(BF)
    pre = dot(first_t[...], hidden, ((1,), (0,)))
    square = pre * pre
    curve = jnp.tanh(ROOT * (pre + 0.044715 * (square * pre)))
    half = 0.5 * (1.0 + curve)
    active = (pre * half).astype(BF)
    out[0] = (hidden.astype(F32) + dot(second_t[...], active, ((1,), (0,)))).astype(BF)
    slope = half + 0.5 * pre * (1.0 - curve * curve) * (ROOT * (1.0 + 0.134145 * square))
    inner = (slope * dot(second[...], cot[0], ((1,), (0,)))).astype(BF)
    back = (cot[0].astype(F32) + dot(first[...], inner, ((1,), (0,)))).astype(BF)
    grad[0] = back
    spec[0] = dot(grid_table, back, ((1,), (1,))).astype(BF)


def mlp(state, cot, synth, table, first, second):
    lats, chans, lons = state.shape
    waves = synth.shape[1]
    hidden = first.shape[1]

    def whole(*shape):
        return pl.BlockSpec(shape, lambda t: (0,) * len(shape))

    def row(*shape):
        return pl.BlockSpec((1,) + shape, lambda t: (t, 0, 0))

    return pl.pallas_call(
        mlp_kernel,
        grid=(lats,),
        in_specs=[
            row(chans, lons),
            row(chans, lons),
            row(waves, chans),
            whole(waves, lons),
            whole(chans, hidden),
            whole(hidden, chans),
            whole(hidden, chans),
            whole(chans, hidden),
        ],
        out_specs=[row(chans, lons), row(chans, lons), row(waves, chans)],
        out_shape=[
            jax.ShapeDtypeStruct((lats, chans, lons), BF),
            jax.ShapeDtypeStruct((lats, chans, lons), BF),
            jax.ShapeDtypeStruct((lats, waves, chans), BF),
        ],
        compiler_params=pltpu.CompilerParams(vmem_limit_bytes=56 << 20),
    )(state, cot, synth, table, first, first.T, second, second.T)


def einsum(form, *values):
    return jnp.einsum(form, *values, preferred_element_type=F32)


def spread_paths(legendre, spec_gain, weights, lats, chan_width):
    spaces, chans = lax.axis_size("space"), lax.axis_size("chan")
    devices = spaces * chans
    table = chan_swap(legendre, 0, 1)
    slots, degrees, lat_count = table.shape
    gains = chan_rows(spec_gain, False)
    real, imag = weights[0], weights[1]
    channels = real.shape[0]
    by_shard = (chans, 1, chan_width, 2 * channels)
    top = jnp.concatenate([real, imag], axis=1).reshape(by_shard)
    low = jnp.concatenate([-imag, real], axis=1).reshape(by_shard)
    mixer = jnp.concatenate([top, low], axis=1).reshape(2 * channels, 2 * channels)
    table_st = table.reshape(slots, degrees, spaces, lats)

    def swap(values):
        return lax.all_to_all(values, BOTH, 0, 0, tiled=True)

    def forward(spectral):
        sent = spectral.reshape(lats, devices, 2 * slots, chan_width).transpose(1, 0, 2, 3)
        got = swap(sent).reshape(spaces, chans, lats, slots, 2, chan_width)
        coeffs = einsum("klst,sytkrc->klyrc", table_st, got).astype(BF)
        coeffs = coeffs.reshape(slots, degrees, 2 * channels)
        mixed = einsum("klx,xo->klo", coeffs, mixer).reshape(slots, degrees, 2, channels)
        mixed = (mixed * gains[None, :, None, :]).astype(BF)
        synth = einsum("klst,klro->sktro", table_st, mixed).astype(BF)
        synth = jnp.broadcast_to(synth[:, None], (spaces, chans) + synth.shape[1:])
        got = swap(synth.reshape((devices, slots) + (lats, 2 * channels)))
        return (
            got.reshape(devices, slots, lats, 2, channels)
            .transpose(2, 0, 1, 3, 4)
            .reshape(lats, devices * slots * 2, channels)
        )

    def backward(part):
        sent = part.reshape(lats, devices, 2 * slots, channels).transpose(1, 0, 2, 3)
        got = swap(sent).reshape(spaces, chans, lats, slots, 2, channels)
        table_sy = jnp.broadcast_to(
            table_st[:, :, :, None], (slots, degrees, spaces, chans, lats)
        )
        coeffs = einsum("klsyt,sytkro->klro", table_sy, got).astype(BF)
        scaled = (coeffs.astype(F32) * gains[None, :, None, :]).astype(BF)
        scaled = scaled.reshape(slots, degrees, 2 * channels)
        mixed = einsum("klo,xo->klx", scaled, mixer).astype(BF)
        mixed = mixed.reshape(slots, degrees, chans, 2, chan_width)
        field = einsum("klst,klyrc->syktrc", table_st, mixed).astype(BF)
        got = swap(field.reshape((devices, slots, lats, 2 * chan_width)))
        return (
            got.reshape(devices, slots, lats, 2, chan_width)
            .transpose(2, 0, 1, 3, 4)
            .reshape(lats, devices * slots * 2, chan_width)
        )

    return forward, backward


def shard_paths(legendre, spec_gain, weights, lats, chan_width):
    chans = lax.axis_size("chan")
    table = lax.all_gather(legendre, "chan", axis=1, tiled=True)
    slots = table.shape[0]
    channels = weights.shape[1]

    def to_orders(values):
        return lax.all_to_all(values, "space", split_axis=1, concat_axis=0, tiled=True)

    def to_bands(values):
        return lax.all_to_all(values, "space", split_axis=0, concat_axis=1, tiled=True)

    def to_degrees(values):
        return lax.all_to_all(values, "chan", split_axis=0, concat_axis=3, tiled=True)

    def to_channels(values):
        return lax.all_to_all(values, "chan", split_axis=3, concat_axis=0, tiled=True)

    def analysis(spectral):
        values = spectral.reshape(lats, -1, 2, chan_width)
        coeffs = einsum("klt,tkrc->lkrc", table, to_orders(values)).astype(BF)
        return to_degrees(coeffs)

    def synthesis(mixed):
        field = einsum("klt,lkrc->tkrc", table, to_channels(mixed.astype(BF))).astype(BF)
        return to_bands(field).reshape(lats, -1, chan_width)

    def forward(spectral):
        coeffs = analysis(spectral)
        products = einsum("lkrc,wco->lkrwo", coeffs, weights)
        real = products[:, :, 0, 0] - products[:, :, 1, 1]
        imag = products[:, :, 0, 1] + products[:, :, 1, 0]
        mixed = jnp.stack([real, imag], axis=2) * spec_gain[:, None, None, :]
        return lax.all_gather(synthesis(mixed), "chan", axis=2, tiled=True)

    def backward(part):
        shaped = part.reshape(part.shape[0], part.shape[1], chans, chan_width)
        pieces = lax.all_to_all(shaped, "chan", split_axis=2, concat_axis=2, tiled=True)
        spectral = jnp.sum(pieces.astype(F32), axis=2).astype(BF)
        coeffs = analysis(spectral)
        scaled = (coeffs.astype(F32) * spec_gain[:, None, None, :]).astype(BF)
        products = einsum("lkro,wco->lkrwc", scaled, weights)
        real = products[:, :, 0, 0] + products[:, :, 1, 1]
        imag = products[:, :, 1, 0] - products[:, :, 0, 1]
        return synthesis(jnp.stack([real, imag], axis=2))

    return forward, backward


def shards(
    state,
    cotangent,
    order_table,
    quad_weight,
    legendre,
    spec_gain,
    spectral_weight,
    mlp_in,
    mlp_out,
):
    lats, chan_width, lon_count = state.shape
    chans = lax.axis_size("chan")
    me = lax.axis_index("chan")
    lon_width = lon_count // chans
    table = transform_table(order_table, lon_count)
    paths = spread_paths if legendre.shape[0] % chans == 0 else shard_paths
    forward, backward = paths(legendre, spec_gain, spectral_weight, lats, chan_width)

    point_state = chan_swap(state, 2, 1)
    first, second = chan_rows(mlp_in, True), chan_rows(mlp_out, True)
    weighting = jnp.repeat(jnp.where(order_table == 0, 1.0, 2.0), 2).astype(BF)
    own_table = lax.dynamic_slice_in_dim(table, me * lon_width, lon_width, 0)
    inverse = (own_table * weighting[None, :]).T

    spectral = einsum("tcn,nj->tjc", state, table)
    spectral = (spectral * quad_weight[:, None, None]).astype(BF)
    synth = forward(spectral)
    output, point_grad, part = mlp(point_state, cotangent, synth, inverse, first, second)
    hidden_grad = chan_swap(point_grad, 1, 2)
    field = backward(part)
    field_grad = einsum("tjc,nj->tcn", field, table) * quad_weight[:, None, None]
    state_grad = (hidden_grad.astype(F32) + field_grad).astype(BF)
    return output, state_grad


def solution(mesh):
    placed = (
        P("space", "chan", None),
        P("space", None, "chan"),
        P(),
        P("space"),
        P("space", "chan", None),
        P("chan", None),
        P(),
        P("chan", None),
        P("chan", None),
    )
    return jax.shard_map(
        shards,
        mesh=mesh,
        in_specs=placed,
        out_specs=(P("space", None, "chan"), P("space", "chan", None)),
        check_vma=False,
    )
```

profile of v0, /device:TPU:1, one launch (start us, length us, event | category | flops | bytes accessed | tf_op | source)
XLA Modules:
  0.0 255.5 jit_solution(13279963913737196121)
XLA Ops:
  1.5 6.1 %fusion.11 = bf16[6,192,256]{2,1,0:T(8,128)(2,1)S(1)} fusion(bf16[6,256,1024]{2,1,0:T(8,128)(2,1)} %param.9, f32[6]{0:T(128)} %param.12, s32[192]{0:T(256)S(1)} %mul.136, s32[192]{0:T(256)S(1)} %get-tuple-element.16, s32[192]{0:T(256)S(1)} %get-tuple-element.17, pred[192]{0:T(512)(128)(4,1)S(1)} %compare_and_fusion), kind=kOutput, calls=%fused_computation.22 | convolution fusion | flops 608501760 | bytes 3738072 | tf_op jit(solution)/shard_map/tcn,nj->tjc/dot_general | solution.py:129
  7.9 0.9 copy.52
  8.8 7.1 %all-to-all-start = ((bf16[32,6,6,256]{3,2,1,0:T(8,128)(2,1)}), bf16[32,6,6,256]{3,2,1,0:T(8,128)(2,1)S(1)}, u32[]{:S(2)}, u32[]{:S(2)}) async-start(bf16[32,6,6,256]{3,2,1,0:T(8,128)(2,1)} %copy.52), calls=%async_computation | async-start | bytes 1572864 | tf_op jit(solution)/shard_map/all_to_all | solution.py:147
  16.6 1.4 collective-permute-start.1
  18.1 0.9 fusion.33
  18.9 0.9 neg.14
  19.8 1.8 maximum_maximum_fusion
  21.8 2.6 %copy.61 = bf16[1024,1024]{1,0:T(8,128)(2,1)} copy(bf16[1024,1024]{0,1:T(8,128)(2,1)S(1)} %bitcast.85) | data formatting | bytes 4194304 | tf_op jit(solution)/shard_map/klx,xo->klo/dot_general | solution.py:129
  24.7 0.9 copy.51
  25.6 0.8 dynamic_update_slice.49
  27.1 0.9 constant_dynamic-update-slice_fusion.5
  28.0 8.9 %all-to-all-done = bf16[32,6,6,256]{3,2,1,0:T(8,128)(2,1)S(1)} async-done(((bf16[32,6,6,256]{3,2,1,0:T(8,128)(2,1)}), bf16[32,6,6,256]{3,2,1,0:T(8,128)(2,1)S(1)}, u32[]{:S(2)}, u32[]{:S(2)}) %all-to-all-start) | async-done | bytes 589856 | tf_op jit(solution)/shard_map/all_to_all | solution.py:147
  37.4 1.4 fusion
  39.5 1.2 reshape.109
  40.7 2.1 fusion.8
  44.2 0.9 reshape.96
  45.0 1.8 copy.64
  46.8 3.4 %all-to-all-start.1 = ((bf16[32,3,6,1024]{3,2,1,0:T(8,128)(2,1)}), bf16[32,3,6,1024]{3,2,1,0:T(8,128)(2,1)}, u32[]{:S(2)}, u32[]{:S(2)}) async-start(bf16[32,3,6,1024]{3,2,1,0:T(8,128)(2,1)} %copy.64), calls=%async_computation.1 | async-start | bytes 3145728 | tf_op jit(solution)/shard_map/all_to_all | solution.py:147
  50.5 3.4 %constant_dynamic-slice_fusion.4 = (bf16[6,256,512]{2,1,0:T(8,128)(2,1)}, bf16[6,512,512]{2,1,0:T(8,128)(2,1)S(1)}) fusion(bf16[6,256,1024]{2,1,0:T(8,128)(2,1)} %param.9, s32[]{:T(128)S(6)} %select_n.131, bf16[6,512,512]{2,1,0:T(8,128)(2,1)S(1)} %broadcast_in_dim.46, s32[]{:T(128)S(6)} %select_n.129, s32[]{:T(128)S(6)} %select_n.127), kind=kLoop, calls=%fused_computation.59 | loop fusion | bytes 6291468 | tf_op jit(solution)/shard_map/dynamic_slice | solution.py:36
  53.9 1.3 collective-permute-start
  55.2 1.2 copy.69
  56.4 0.9 constant_dynamic-slice_fusion
  57.5 1.9 copy.67
  59.4 1.6 constant_dynamic-slice_fusion.1
  61.0 1.3 collective-permute-start.3
  63.0 0.9 convert_element_type.68
  63.9 0.9 broadcast_in_dim.54
  65.7 4.4 %multiply_convert_fusion = bf16[1024,192]{0,1:T(8,128)(2,1)S(1)} fusion(s32[192]{0:T(256)S(1)} %mul.136, s32[192]{0:T(256)S(1)} %get-tuple-element.16, s32[192]{0:T(256)S(1)} %get-tuple-element.17, pred[192]{0:T(512)(128)(4,1)} %copy-done.18), kind=kLoop, calls=%fused_computation.30 | loop fusion | flops 3932160 | bytes 395712 | tf_op jit(solution)/shard_map/convert_element_type | solution.py:23
  70.9 37.6 %collective-permute-done.5 = bf16[192,512]{0,1:T(8,128)(2,1)} collective-permute-done((bf16[192,512]{0,1:T(8,128)(2,1)}, bf16[192,512]{0,1:T(8,128)(2,1)}, u32[]{:S(2)}, u32[]{:S(2)}) %collective-permute-start.5) | collective-permute-done | bytes 196640 | tf_op jit(solution)/shard_map/ppermute | solution.py:59
  108.5 1.6 collective-permute-start.6
  110.0 2.7 %collective-permute-done.3 = bf16[128,768]{0,1:T(8,128)(2,1)} collective-permute-done((bf16[128,768]{0,1:T(8,128)(2,1)}, bf16[128,768]{0,1:T(8,128)(2,1)}, u32[]{:S(2)}, u32[]{:S(2)}) %collective-permute-start.3) | collective-permute-done | bytes 196640 | tf_op jit(solution)/shard_map/ppermute | solution.py:59
  112.7 1.0 collective-permute-start.4
  113.7 0.9 broadcast_in_dim.53
  115.4 3.2 %dynamic_update_slice.56 = bf16[768,512]{0,1:T(8,128)(2,1)} dynamic-update-slice(bf16[768,512]{0,1:T(8,128)(2,1)} %constant_dynamic-update-slice_fusion.1, bf16[192,512]{0,1:T(8,128)(2,1)} %collective-permute-done.5, s32[]{:T(128)S(6)} %select_n.150, s32[]{:T(128)} %constant.105.clone.1) | dynamic-update-slice | bytes 393220 | tf_op jit(solution)/shard_map/dynamic_update_slice | solution.py:62
  118.6 1.6 constant_dynamic-update-slice_fusion.3
  120.3 3.3 %dynamic_update_slice.57 = bf16[768,512]{0,1:T(8,128)(2,1)} dynamic-update-slice(bf16[768,512]{0,1:T(8,128)(2,1)} %dynamic_update_slice.56, bf16[192,512]{0,1:T(8,128)(2,1)S(1)} %collective-permute-done.6, s32[]{:T(128)S(6)} %select_n.151, s32[]{:T(128)} %constant.105.clone.1) | dynamic-update-slice | bytes 393220 | tf_op jit(solution)/shard_map/dynamic_update_slice | solution.py:65
  123.6 2.4 copy.72.second
  126.0 1.6 constant_dynamic-update-slice_fusion.2
  127.6 2.3 copy.71.first
  130.0 1.6 constant_dynamic-update-slice_fusion.7.state
  131.6 4.8 %reshape.120 = bf16[32,3,6,2,512]{4,3,2,1,0:T(2,128)(2,1)} reshape(bf16[32,3,6,1024]{3,2,1,0:T(8,128)(2,1)} %all-to-all-done.1) | data formatting | bytes 2359296 | tf_op jit(solution)/shard_map/reshape | solution.py:160
  136.4 3.1 %copy.66 = bf16[6,32,3,2,512]{4,3,2,1,0:T(2,128)(2,1)} copy(bf16[6,32,3,2,512]{4,3,0,2,1:T(2,128)(2,1)} %bitcast.90) | data formatting | bytes 2359296 | tf_op jit(solution)/shard_map/transpose | solution.py:161
  139.5 3.7 %reshape.98.synth = bf16[6,192,512]{2,1,0:T(8,128)(2,1)} reshape(bf16[6,32,3,2,512]{4,3,2,1,0:T(2,128)(2,1)} %copy.66) | data formatting | bytes 2359296 | tf_op jit(solution)/shard_map/reshape | solution.py:162
  143.2 18.8 %shard_map.104 = (bf16[6,512,512]{2,1,0:T(8,128)(2,1)}, bf16[6,512,512]{2,1,0:T(8,128)(2,1)}, bf16[6,192,512]{2,1,0:T(8,128)(2,1)}) custom-call(bf16[6,512,512]{2,1,0:T(8,128)(2,1)} %copy-done, bf16[6,512,512]{2,1,0:T(8,128)(2,1)} %cot.1, bf16[6,192,512]{2,1,0:T(8,128)(2,1)} %reshape.98.synth, bf16[192,512]{1,0:T(8,128)(2,1)} %multiply_bitcast_fusion.table, ...), custom_call_target="tpu_custom_call" | custom-call | tf_op jit(solution)/shard_map/pallas_call | solution.py:105
  162.1 2.2 reshape.99
  164.3 1.4 copy.74
  165.7 4.9 %all-to-all-start.2 = ((bf16[32,6,6,512]{3,2,1,0:T(8,128)(2,1)}), bf16[32,6,6,512]{3,2,1,0:T(8,128)(2,1)S(1)}, u32[]{:S(2)}, u32[]{:S(2)}) async-start(bf16[32,6,6,512]{3,2,1,0:T(8,128)(2,1)} %copy.74), calls=%async_computation.2 | async-start | bytes 3145728 | tf_op jit(solution)/shard_map/all_to_all | solution.py:147
  171.1 1.5 copy-done.5
  172.5 1.5 constant_dynamic-slice_fusion.5
  174.0 1.7 copy-done.3
  175.7 1.4 collective-permute-start.7
  177.1 30.0 %all-to-all-done.2 = bf16[32,6,6,512]{3,2,1,0:T(8,128)(2,1)S(1)} async-done(((bf16[32,6,6,512]{3,2,1,0:T(8,128)(2,1)}), bf16[32,6,6,512]{3,2,1,0:T(8,128)(2,1)S(1)}, u32[]{:S(2)}, u32[]{:S(2)}) %all-to-all-start.2) | async-done | bytes 1179680 | tf_op jit(solution)/shard_map/all_to_all | solution.py:147
  207.1 1.0 reshape.121
  208.1 0.8 fusion.10
  211.3 1.4 copy.107
  212.7 2.8 %reshape.122 = bf16[32,3,6,512]{3,2,1,0:T(8,128)(2,1)} reshape(bf16[16,2,3,6,2,256]{5,4,3,2,1,0:T(2,128)(2,1)} %copy.107) | data formatting | bytes 1179648 | tf_op jit(solution)/shard_map/reshape | solution.py:177
  215.5 4.6 %all-to-all-start.3 = ((bf16[32,3,6,512]{3,2,1,0:T(8,128)(2,1)}), bf16[32,3,6,512]{3,2,1,0:T(8,128)(2,1)}, u32[]{:S(2)}, u32[]{:S(2)}) async-start(bf16[32,3,6,512]{3,2,1,0:T(8,128)(2,1)} %reshape.122), calls=%async_computation.3 | async-start | bytes 1572864 | tf_op jit(solution)/shard_map/all_to_all | solution.py:147
  220.1 3.3 %collective-permute-done.7 = bf16[6,256,512]{2,1,0:T(8,128)(2,1)} collective-permute-done((bf16[6,256,512]{2,1,0:T(8,128)(2,1)}, bf16[6,256,512]{2,1,0:T(8,128)(2,1)}, u32[]{:S(2)}, u32[]{:S(2)}) %collective-permute-start.7) | collective-permute-done | bytes 1572896 | tf_op jit(solution)/shard_map/ppermute | solution.py:39
  223.4 1.7 constant_dynamic-update-slice_fusion
  225.1 16.1 %all-to-all-done.3 = bf16[32,3,6,512]{3,2,1,0:T(8,128)(2,1)} async-done(((bf16[32,3,6,512]{3,2,1,0:T(8,128)(2,1)}), bf16[32,3,6,512]{3,2,1,0:T(8,128)(2,1)}, u32[]{:S(2)}, u32[]{:S(2)}) %all-to-all-start.3) | async-done | bytes 589856 | tf_op jit(solution)/shard_map/all_to_all | solution.py:147
  241.1 2.7 %reshape.123 = bf16[32,3,6,2,256]{4,3,2,1,0:T(2,128)(2,1)} reshape(bf16[32,3,6,512]{3,2,1,0:T(8,128)(2,1)} %all-to-all-done.3) | data formatting | bytes 1179648 | tf_op jit(solution)/shard_map/reshape | solution.py:179
  243.8 2.3 copy.83
  246.1 2.6 %reshape.105 = bf16[6,192,256]{2,1,0:T(8,128)(2,1)} reshape(bf16[6,32,3,2,256]{4,3,2,1,0:T(2,128)(2,1)} %copy.83) | data formatting | bytes 1179648 | tf_op jit(solution)/shard_map/reshape | solution.py:181
  248.8 6.7 %add_convert_fusion = bf16[6,256,1024]{2,1,0:T(8,128)(2,1)} fusion(bf16[6,256,1024]{2,1,0:T(8,128)(2,1)S(1)} %constant_dynamic-update-slice_fusion, f32[6]{0:T(128)S(1)} %copy-done.17, bf16[6,192,256]{2,1,0:T(8,128)(2,1)} %reshape.105, s32[192]{0:T(256)S(1)} %mul.136, s32[192]{0:T(256)S(1)} %get-tuple-element.16, s32[192]{0:T(256)S(1)} %get-tuple-element.17, ...), kind=kOutput, calls=%fused_computation | convolution fusion | flops 614203392 | bytes 6883800 | tf_op jit(solution)/shard_map/tjc,nj->tcn/dot_general | solution.py:129
  (74 shorter events, 11.7 us)
Async XLA Ops:
  0.7 0.9 copy-start.18
  7.7 8.3 %copy-start.15 = (bf16[6,48,96]{2,1,0:T(8,128)(2,1)S(1)}, bf16[6,48,96]{2,1,0:T(8,128)(2,1)}, u32[]{:S(2)}) copy-start(bf16[6,48,96]{2,1,0:T(8,128)(2,1)} %param.13) | copy-start | bytes 165892
  7.7 10.3 %copy-start.14 = (f32[48,512]{1,0:T(8,128)S(1)}, f32[48,512]{1,0:T(8,128)}, u32[]{:S(2)}) copy-start(f32[48,512]{1,0:T(8,128)} %param.14) | copy-start | bytes 294916
  7.7 10.4 %copy-start.10 = (bf16[2,512,512]{2,1,0:T(8,128)(2,1)S(1)}, bf16[2,512,512]{2,1,0:T(8,128)(2,1)}, u32[]{:S(2)}) copy-start(bf16[2,512,512]{2,1,0:T(8,128)(2,1)} %param.15) | copy-start | bytes 3145732
  8.8 28.1 %all-to-all-start = ((bf16[32,6,6,256]{3,2,1,0:T(8,128)(2,1)}), bf16[32,6,6,256]{3,2,1,0:T(8,128)(2,1)S(1)}, u32[]{:S(2)}, u32[]{:S(2)}) async-start(bf16[32,6,6,256]{3,2,1,0:T(8,128)(2,1)} %copy.52), calls=%async_computation | async-start | bytes 1572864 | tf_op jit(solution)/shard_map/all_to_all | solution.py:147
  16.6 8.1 %collective-permute-start.1 = (bf16[3,48,96]{2,1,0:T(8,128)(2,1)}, bf16[3,48,96]{2,1,0:T(8,128)(2,1)}, u32[]{:S(2)}, u32[]{:S(2)}) collective-permute-start(bf16[3,48,96]{2,1,0:T(8,128)(2,1)} %get-tuple-element.14), channel_id=1, source_target_pairs={{0,1},{1,0},{2,3},{3,2},{4,5},{5,4},{6,7},{7,6},{8,9},{9,8},{10,11... | collective-permute-start | bytes 82952 | tf_op jit(solution)/shard_map/ppermute | solution.py:39
  17.9 9.1 %collective-permute-start.2 = (f32[48,512]{1,0:T(8,128)S(1)}, f32[48,512]{1,0:T(8,128)}, u32[]{:S(2)}, u32[]{:S(2)}) collective-permute-start(f32[48,512]{1,0:T(8,128)S(1)} %copy-done.14), channel_id=1, source_target_pairs={{0,1},{1,0},{2,3},{3,2},{4,5},{5,4},{6,7},{7,6},{8,9},{9,8},{10,11... | collective-permute-start | bytes 294920 | tf_op jit(solution)/shard_map/ppermute | solution.py:59
  21.6 2.8 %copy-start.1 = (bf16[2,2,256,1024]{3,2,1,0:T(8,128)(2,1)}, bf16[2,2,256,1024]{3,2,1,0:T(8,128)(2,1)S(1)}, u32[]{:S(2)}) copy-start(bf16[2,2,256,1024]{3,2,1,0:T(8,128)(2,1)S(1)} %maximum_maximum_fusion) | copy-start | bytes 6291460
  28.0 8.9 %copy-start.11 = (f32[96,512]{1,0:T(8,128)}, f32[96,512]{1,0:T(8,128)S(1)}, u32[]{:S(2)}) copy-start(f32[96,512]{1,0:T(8,128)S(1)} %constant_dynamic-update-slice_fusion.5) | copy-start | bytes 589828
  37.4 3.3 %copy-start.7 = (bf16[1024,1024]{1,0:T(8,128)(2,1)S(1)}, bf16[1024,1024]{1,0:T(8,128)(2,1)}, u32[]{:S(2)}) copy-start(bf16[1024,1024]{1,0:T(8,128)(2,1)} %copy.61) | copy-start | bytes 6291460
  37.4 3.3 %copy-start.8 = (bf16[3,96,16,6]{1,3,2,0:T(8,128)(2,1)S(1)}, bf16[3,96,16,6]{1,3,2,0:T(8,128)(2,1)}, u32[]{:S(2)}) copy-start(bf16[3,96,16,6]{1,3,2,0:T(8,128)(2,1)} %reshape.91) | copy-start | bytes 165892
  38.8 1.9 copy-start.12
  46.8 84.7 %all-to-all-start.1 = ((bf16[32,3,6,1024]{3,2,1,0:T(8,128)(2,1)}), bf16[32,3,6,1024]{3,2,1,0:T(8,128)(2,1)}, u32[]{:S(2)}, u32[]{:S(2)}) async-start(bf16[32,3,6,1024]{3,2,1,0:T(8,128)(2,1)} %copy.64), calls=%async_computation.1 | async-start | bytes 3145728 | tf_op jit(solution)/shard_map/all_to_all | solution.py:147
  53.9 8.4 %copy-start.16 = (s32[96]{0:T(128)S(1)}, s32[96]{0:T(128)}, u32[]{:S(2)}) copy-start(s32[96]{0:T(128)} %param.11) | copy-start | bytes 1156
  53.9 76.0 %collective-permute-start = (bf16[6,256,512]{2,1,0:T(8,128)(2,1)}, bf16[6,256,512]{2,1,0:T(8,128)(2,1)}, u32[]{:S(2)}, u32[]{:S(2)}) collective-permute-start(bf16[6,256,512]{2,1,0:T(8,128)(2,1)} %get-tuple-element.10), channel_id=1, source_target_pairs={{0,1},{1,0},{2,3},{3,2},{4,5},{5,4},{6,7},{7,6},{8,9},{9,8},{10,11... | collective-permute-start | bytes 4718600 | tf_op jit(solution)/shard_map/ppermute | solution.py:39
  57.3 51.2 %collective-permute-start.5 = (bf16[192,512]{0,1:T(8,128)(2,1)}, bf16[192,512]{0,1:T(8,128)(2,1)}, u32[]{:S(2)}, u32[]{:S(2)}) collective-permute-start(bf16[192,512]{0,1:T(8,128)(2,1)} %constant_dynamic-slice_fusion), channel_id=1, source_target_pairs={{0,1},{1,0},{2,3},{3,2},{4,5},{5,4},{6,7},{7,6},{8,9},{9,8},{10,11... | collective-permute-start | bytes 589832 | tf_op jit(solution)/shard_map/ppermute | solution.py:59
  61.0 51.7 %collective-permute-start.3 = (bf16[128,768]{0,1:T(8,128)(2,1)}, bf16[128,768]{0,1:T(8,128)(2,1)}, u32[]{:S(2)}, u32[]{:S(2)}) collective-permute-start(bf16[128,768]{0,1:T(8,128)(2,1)} %constant_dynamic-slice_fusion.1), channel_id=1, source_target_pairs={{0,1},{1,0},{2,3},{3,2},{4,5},{5,4},{6,7},{7,6},{8,9},{9,8},{10,11... | collective-permute-start | bytes 589832 | tf_op jit(solution)/shard_map/ppermute | solution.py:59
  63.9 50.7 %copy-start.6 = (bf16[256,768]{0,1:T(8,128)(2,1)S(1)}, bf16[256,768]{0,1:T(8,128)(2,1)}, u32[]{:S(2)}) copy-start(bf16[256,768]{0,1:T(8,128)(2,1)} %copy.67) | copy-start | bytes 1179652
  108.5 11.8 %collective-permute-start.6 = (bf16[192,512]{0,1:T(8,128)(2,1)}, bf16[192,512]{0,1:T(8,128)(2,1)S(1)}, u32[]{:S(2)}, u32[]{:S(2)}) collective-permute-start(bf16[192,512]{0,1:T(8,128)(2,1)} %collective-permute-done.5), channel_id=1, source_target_pairs={{0,2},{2,0},{4,6},{6,4},{8,10},{10,8},{12,14},{14,12},{16,18},{18,... | collective-permute-start | bytes 589832 | tf_op jit(solution)/shard_map/ppermute | solution.py:61
  112.7 13.3 %collective-permute-start.4 = (bf16[128,768]{0,1:T(8,128)(2,1)}, bf16[128,768]{0,1:T(8,128)(2,1)}, u32[]{:S(2)}, u32[]{:S(2)}) collective-permute-start(bf16[128,768]{0,1:T(8,128)(2,1)} %collective-permute-done.3), channel_id=1, source_target_pairs={{0,2},{2,0},{4,6},{6,4},{8,10},{10,8},{12,14},{14,12},{16,18},{18,... | collective-permute-start | bytes 589832 | tf_op jit(solution)/shard_map/ppermute | solution.py:61
  131.5 8.0 %copy-start = (bf16[6,512,512]{2,1,0:T(8,128)(2,1)}, bf16[6,512,512]{2,1,0:T(8,128)(2,1)S(1)}, u32[]{:S(2)}) copy-start(bf16[6,512,512]{2,1,0:T(8,128)(2,1)S(1)} %constant_dynamic-update-slice_fusion.7.state) | copy-start | bytes 9437188
  165.7 4.9 %copy-start.9 = (bf16[3,96,16,6]{1,3,2,0:T(8,128)(2,1)S(1)}, bf16[3,96,16,6]{1,3,2,0:T(8,128)(2,1)}, u32[]{:S(2)}) copy-start(bf16[3,96,16,6]{1,3,2,0:T(8,128)(2,1)} %reshape.91) | copy-start | bytes 165892
  165.7 41.4 %all-to-all-start.2 = ((bf16[32,6,6,512]{3,2,1,0:T(8,128)(2,1)}), bf16[32,6,6,512]{3,2,1,0:T(8,128)(2,1)S(1)}, u32[]{:S(2)}, u32[]{:S(2)}) async-start(bf16[32,6,6,512]{3,2,1,0:T(8,128)(2,1)} %copy.74), calls=%async_computation.2 | async-start | bytes 3145728 | tf_op jit(solution)/shard_map/all_to_all | solution.py:147
  170.6 1.9 copy-start.5
  174.0 1.7 copy-start.3
  174.0 34.0 %copy-start.13 = (f32[96,512]{1,0:T(8,128)S(1)}, f32[96,512]{1,0:T(8,128)}, u32[]{:S(2)}) copy-start(f32[96,512]{1,0:T(8,128)} %copy-done.11) | copy-start | bytes 589828
  175.7 47.7 %collective-permute-start.7 = (bf16[6,256,512]{2,1,0:T(8,128)(2,1)}, bf16[6,256,512]{2,1,0:T(8,128)(2,1)}, u32[]{:S(2)}, u32[]{:S(2)}) collective-permute-start(bf16[6,256,512]{2,1,0:T(8,128)(2,1)} %get-tuple-element.8), channel_id=1, source_target_pairs={{0,1},{1,0},{2,3},{3,2},{4,5},{5,4},{6,7},{7,6},{8,9},{9,8},{10,11... | collective-permute-start | bytes 4718600 | tf_op jit(solution)/shard_map/ppermute | solution.py:39
  208.1 1.6 copy-start.2
  211.3 12.1 %copy-start.4 = (bf16[6,256,1024]{2,1,0:T(8,128)(2,1)S(1)}, bf16[6,256,1024]{2,1,0:T(8,128)(2,1)}, u32[]{:S(2)}) copy-start(bf16[6,256,1024]{2,1,0:T(8,128)(2,1)} %copy-done.3) | copy-start | bytes 9437188
  215.5 25.7 %all-to-all-start.3 = ((bf16[32,3,6,512]{3,2,1,0:T(8,128)(2,1)}), bf16[32,3,6,512]{3,2,1,0:T(8,128)(2,1)}, u32[]{:S(2)}, u32[]{:S(2)}) async-start(bf16[32,3,6,512]{3,2,1,0:T(8,128)(2,1)} %reshape.122), calls=%async_computation.3 | async-start | bytes 1572864 | tf_op jit(solution)/shard_map/all_to_all | solution.py:147
  225.0 23.7 %copy-start.17 = (f32[6]{0:T(128)S(1)}, f32[6]{0:T(128)}, u32[]{:S(2)}) copy-start(f32[6]{0:T(128)} %param.12) | copy-start | bytes 76
  225.1 23.7 %copy-start.19 = (pred[192]{0:T(512)(128)(4,1)S(1)}, pred[192]{0:T(512)(128)(4,1)}, u32[]{:S(2)}) copy-start(pred[192]{0:T(512)(128)(4,1)} %copy-done.18) | copy-start | bytes 580
where the time goes:
time: 257 us; the launch traced here: 256 us
  waiting for transfers between devices  98.6 us (38%)
  local copies, waits for them, and re-layouts  82.6 us (32%)
  starting transfers between devices  28.1 us (11%)
  Pallas kernels  18.8 us (7%)
  matrix products  18.4 us (7%)
  other arithmetic  7.86 us (3%)
    all_to_all x4, waiting for transfers between devices, swap(): return lax.all_to_all(values, BOTH, 0, 0, tiled=True)  55 us
    ppermute x3, waiting for transfers between devices, chan_rows(): piece = lax.ppermute(mine, 'chan', ring)  40.3 us
    all_to_all x4, starting transfers between devices, swap(): return lax.all_to_all(values, BOTH, 0, 0, tiled=True)  20 us
    pallas_call x1, Pallas kernels, mlp(): pl.pallas_call(mlp_kernel, grid=(lats,), in_specs=[row(chans, lons), row(...  18.8 us
    dot_general x7, matrix products, einsum(): return jnp.einsum(form, *values, preferred_element_type=F32)  18.4 us
    dynamic_update_slice x4, local copies, waits for them, and re-layouts, chan_rows(): lax.dynamic_update_slice_in_dim(result, other, source * rows + (1 - parit...  9.64 us
    unnamed x42, local copies, waits for them, and re-layouts  7 us
    dynamic_slice x4, local copies, waits for them, and re-layouts, chan_swap(): lax.dynamic_slice_in_dim(values, (me + shift) % count * width, width, spl...  5.63 us
  transfers between devices with their start and end apart: 12, of which 6 were waited for; matrix products, arithmetic and copies ran while one was open for 22% of the time, Pallas kernels for 0%

commit v1 on v0

--- a/solution.py
+++ b/solution.py
@@ -7,6 +7,7 @@
 from jax.experimental import pallas as pl
 from jax.experimental.pallas import tpu as pltpu
 from jax.sharding import PartitionSpec as P
+
 
 BF = jnp.bfloat16
 F32 = jnp.float32
@@ -39,6 +40,27 @@
             piece = lax.ppermute(piece, "chan", ring)
         source = (me - shift + count) % count
         result = lax.dynamic_update_slice_in_dim(result, piece, source * depth, concat_axis)
+    return result
+
+
+def chan_swap_early(values, split_axis, concat_axis, early):
+    me = lax.axis_index("chan")
+    width = values.shape[split_axis] // 2
+    depth = values.shape[concat_axis]
+    shape = list(values.shape)
+    shape[split_axis] = width
+    shape[concat_axis] = depth * 2
+    own = lax.dynamic_slice_in_dim(values, me * width, width, split_axis)
+    result = jnp.zeros(shape, values.dtype)
+    result = lax.dynamic_update_slice_in_dim(result, own, me * depth, concat_axis)
+    spans = ((0, early), (early, values.shape[0]))
+    for low, high in spans:
+        rows = lax.slice_in_dim(values, low, high, axis=0)
+        piece = lax.dynamic_slice_in_dim(rows, (1 - me) * width, width, split_axis)
+        piece = lax.ppermute(piece, "chan", [(0, 1), (1, 0)])
+        start = [0] * values.ndim
+        start[0], start[concat_axis] = low, (1 - me) * depth
+        result = lax.dynamic_update_slice(result, piece, start)
     return result
 
 
@@ -74,9 +96,24 @@
     return lax.dot_general(left, right, (dims, ((), ())), preferred_element_type=F32)
 
 
-def mlp_kernel(state, cot, synth, table, first, first_t, second, second_t, out, grad, spec):
+def pick(base, rows, first):
+    lanes = lax.broadcasted_iota(jnp.int32, (base.shape[0], rows), 1)
+    return jnp.where(lanes == base[:, :1] + first, 1.0, 0.0).astype(BF)
+
+
+def mlp_kernel(
+    regroup, state, cot, synth, table, base, place, first, first_t, second, second_t,
+    out, grad, spec, parts,
+):
     grid_table = table[...]
-    wave = dot(synth[0], grid_table, ((0,), (0,)))
+    step = pl.program_id(0)
+    lats = pl.num_programs(0)
+    if regroup:
+        rows = pick(base[...], synth.shape[0], step * regroup)
+        waves = dot(rows, synth[...], ((1,), (0,))).astype(BF)
+    else:
+        waves = synth[0]
+    wave = dot(waves, grid_table, ((0,), (0,)))
     hidden = (state[0].astype(F32) + wave).astype(BF)
     pre = dot(first_t[...], hidden, ((1,), (0,)))
     square = pre * pre
@@ -88,41 +125,130 @@
     inner = (slope * dot(second[...], cot[0], ((1,), (0,)))).astype(BF)
     back = (cot[0].astype(F32) + dot(first[...], inner, ((1,), (0,)))).astype(BF)
     grad[0] = back
-    spec[0] = dot(grid_table, back, ((1,), (1,))).astype(BF)
-
-
-def mlp(state, cot, synth, table, first, second):
+    part = dot(grid_table, back, ((1,), (1,))).astype(BF)
+    if regroup:
+        parts[step] = part
+
+        @pl.when(step == lats - 1)
+        def _():
+            flat = parts[...].reshape(-1, part.shape[1])
+            spec[...] = dot(place[...], flat, ((1,), (0,))).astype(BF)
+    else:
+        spec[0] = part
+
+
+def whole(shape):
+    return pl.BlockSpec(shape, lambda t: (0,) * len(shape))
+
+
+def row(*shape):
+    return pl.BlockSpec((1,) + shape, lambda t: (t, 0, 0))
+
+
+def mlp(state, cot, synth, table, base, place, regroup, first, second):
     lats, chans, lons = state.shape
-    waves = synth.shape[1]
-    hidden = first.shape[1]
-
-    def whole(*shape):
-        return pl.BlockSpec(shape, lambda t: (0,) * len(shape))
-
-    def row(*shape):
-        return pl.BlockSpec((1,) + shape, lambda t: (t, 0, 0))
-
+    waves = table.shape[0]
+    operands = (table, base, place, first, first.T, second, second.T)
+    wave_spec = whole(synth.shape) if regroup else row(waves, chans)
+    wave_shape = synth.shape if regroup else (lats, waves, chans)
     return pl.pallas_call(
-        mlp_kernel,
+        functools.partial(mlp_kernel, regroup),
         grid=(lats,),
-        in_specs=[
-            row(chans, lons),
-            row(chans, lons),
-            row(waves, chans),
-            whole(waves, lons),
-            whole(chans, hidden),
-            whole(hidden, chans),
-            whole(hidden, chans),
-            whole(chans, hidden),
-        ],
-        out_specs=[row(chans, lons), row(chans, lons), row(waves, chans)],
+        in_specs=[row(chans, lons), row(chans, lons), wave_spec]
+        + [whole(value.shape) for value in operands],
+        out_specs=[row(chans, lons), row(chans, lons), wave_spec],
         out_shape=[
             jax.ShapeDtypeStruct((lats, chans, lons), BF),
             jax.ShapeDtypeStruct((lats, chans, lons), BF),
-            jax.ShapeDtypeStruct((lats, waves, chans), BF),
+            jax.ShapeDtypeStruct(wave_shape, BF),
         ],
+        scratch_shapes=[pltpu.VMEM((lats, waves, chans) if regroup else (1, 16, 128), BF)],
         compiler_params=pltpu.CompilerParams(vmem_limit_bytes=56 << 20),
-    )(state, cot, synth, table, first, first.T, second, second.T)
+    )(state, cot, synth, *operands)
+
+
+def last_kernel(regroup, quad, hidden_grad, field, table, base, out):
+    step = pl.program_id(0)
+    rows = pick(base[...], field.shape[0], step * regroup)
+    waves = dot(rows, field[...], ((1,), (0,))).astype(BF)
+    wave = dot(waves, table[...], ((0,), (0,)))
+    out[0] = (hidden_grad[0].astype(F32) + wave * quad[step]).astype(BF)
+
+
+def last(quad, hidden_grad, field, table, base, regroup):
+    lats, chans, lons = hidden_grad.shape
+    return pl.pallas_call(
+        functools.partial(last_kernel, regroup),
+        grid=(lats,),
+        in_specs=[pl.BlockSpec(memory_space=pltpu.SMEM), row(chans, lons)]
+        + [whole(value.shape) for value in (field, table, base)],
+        out_specs=row(chans, lons),
+        out_shape=jax.ShapeDtypeStruct(hidden_grad.shape, BF),
+        compiler_params=pltpu.CompilerParams(vmem_limit_bytes=40 << 20),
+    )(quad, hidden_grad, field, table, base)
+
+
+def expand(table, base, lines):
+    slots = table.shape[0]
+    return jnp.concatenate(
+        [
+            dot(table[k], pick(base, lines, 2 * k + r), ((1,), (0,))).astype(BF)
+            for r in range(2)
+            for k in range(slots)
+        ],
+        axis=0,
+    )
+
+
+def ahead_kernel(got, table, base, gain, weights, out):
+    spaces, chans, rows, width = got.shape
+    matrix = expand(table, base[...], spaces * rows)
+    pieces = [got[:, y].reshape(spaces * rows, width) for y in range(chans)]
+    coeffs = jnp.concatenate(
+        [dot(matrix, piece, ((1,), (0,))).astype(BF) for piece in pieces], axis=1
+    )
+    count = coeffs.shape[0] // 2
+    real, imag = coeffs[:count], coeffs[count:]
+    left, right = weights[0], weights[1]
+    flat = ((1,), (0,))
+    gains = jnp.concatenate([gain[...]] * table.shape[0], axis=0)
+    top = ((dot(real, left, flat) - dot(imag, right, flat)) * gains).astype(BF)
+    low = ((dot(real, right, flat) + dot(imag, left, flat)) * gains).astype(BF)
+    mixed = jnp.concatenate([top, low], axis=0)
+    synth = dot(matrix, mixed, ((0,), (0,))).astype(BF).reshape(spaces, rows, -1)
+    for y in range(chans):
+        out[:, y] = synth
+
+
+def behind_kernel(got, table, base, gain, weights, out):
+    spaces, chans, rows, channels = got.shape
+    matrix = expand(table, base[...], spaces * rows)
+    total = None
+    for y in range(chans):
+        term = dot(matrix, got[:, y].reshape(spaces * rows, channels), ((1,), (0,)))
+        total = term if total is None else total + term
+    coeffs = total.astype(BF).astype(F32)
+    count = coeffs.shape[0] // 2
+    gains = jnp.concatenate([gain[...]] * table.shape[0], axis=0)
+    real = (coeffs[:count] * gains).astype(BF)
+    imag = (coeffs[count:] * gains).astype(BF)
+    left, right = weights[0], weights[1]
+    flat = ((1,), (1,))
+    top = (dot(real, left, flat) + dot(imag, right, flat)).astype(BF)
+    low = (dot(imag, left, flat) - dot(real, right, flat)).astype(BF)
+    mixed = jnp.concatenate([top, low], axis=0)
+    field = dot(matrix, mixed, ((0,), (0,))).astype(BF).reshape(spaces, rows, channels)
+    width = channels // chans
+    for y in range(chans):
+        out[:, y] = field[:, :, y * width : (y + 1) * width]
+
+
+def stage(kernel, got, table, base, gain, weights, width):
+    return pl.pallas_call(
+        kernel,
+        out_shape=jax.ShapeDtypeStruct(got.shape[:3] + (width,), BF),
+        compiler_params=pltpu.CompilerParams(vmem_limit_bytes=48 << 20),
+    )(got, table, base, gain, weights)
 
 
 def einsum(form, *values):
@@ -133,62 +259,47 @@
     spaces, chans = lax.axis_size("space"), lax.axis_size("chan")
     devices = spaces * chans
     table = chan_swap(legendre, 0, 1)
-    slots, degrees, lat_count = table.shape
+    slots, _, lat_count = table.shape
     gains = chan_rows(spec_gain, False)
-    real, imag = weights[0], weights[1]
-    channels = real.shape[0]
-    by_shard = (chans, 1, chan_width, 2 * channels)
-    top = jnp.concatenate([real, imag], axis=1).reshape(by_shard)
-    low = jnp.concatenate([-imag, real], axis=1).reshape(by_shard)
-    mixer = jnp.concatenate([top, low], axis=1).reshape(2 * channels, 2 * channels)
-    table_st = table.reshape(slots, degrees, spaces, lats)
+    channels = weights.shape[1]
+    lines = lats * slots * 2
+    rows = -(-lines // 8) * 8
+    lat = jnp.arange(lat_count, dtype=jnp.int32)
+    spot = lat // lats * rows + lat % lats * (2 * slots)
+    spot = jnp.broadcast_to(spot[:, None], (lat_count, 128))
 
     def swap(values):
-        return lax.all_to_all(values, BOTH, 0, 0, tiled=True)
+        flat = values.reshape((devices,) + values.shape[-2:])
+        return lax.all_to_all(flat, BOTH, 0, 0, tiled=True)
+
+    def parted(values):
+        return values.reshape((spaces, chans) + values.shape[1:])
 
     def forward(spectral):
         sent = spectral.reshape(lats, devices, 2 * slots, chan_width).transpose(1, 0, 2, 3)
-        got = swap(sent).reshape(spaces, chans, lats, slots, 2, chan_width)
-        coeffs = einsum("klst,sytkrc->klyrc", table_st, got).astype(BF)
-        coeffs = coeffs.reshape(slots, degrees, 2 * channels)
-        mixed = einsum("klx,xo->klo", coeffs, mixer).reshape(slots, degrees, 2, channels)
-        mixed = (mixed * gains[None, :, None, :]).astype(BF)
-        synth = einsum("klst,klro->sktro", table_st, mixed).astype(BF)
-        synth = jnp.broadcast_to(synth[:, None], (spaces, chans) + synth.shape[1:])
-        got = swap(synth.reshape((devices, slots) + (lats, 2 * channels)))
-        return (
-            got.reshape(devices, slots, lats, 2, channels)
-            .transpose(2, 0, 1, 3, 4)
-            .reshape(lats, devices * slots * 2, channels)
-        )
+        sent = sent.reshape(devices, lines, chan_width)
+        sent = jnp.pad(sent, [(0, 0), (0, rows - lines), (0, 0)])
+        got = swap(sent)
+        synth = stage(ahead_kernel, parted(got), table, spot, gains, weights, channels)
+        return swap(synth).reshape(devices * rows, channels)
 
     def backward(part):
-        sent = part.reshape(lats, devices, 2 * slots, channels).transpose(1, 0, 2, 3)
-        got = swap(sent).reshape(spaces, chans, lats, slots, 2, channels)
-        table_sy = jnp.broadcast_to(
-            table_st[:, :, :, None], (slots, degrees, spaces, chans, lats)
-        )
-        coeffs = einsum("klsyt,sytkro->klro", table_sy, got).astype(BF)
-        scaled = (coeffs.astype(F32) * gains[None, :, None, :]).astype(BF)
-        scaled = scaled.reshape(slots, degrees, 2 * channels)
-        mixed = einsum("klo,xo->klx", scaled, mixer).astype(BF)
-        mixed = mixed.reshape(slots, degrees, chans, 2, chan_width)
-        field = einsum("klst,klyrc->syktrc", table_st, mixed).astype(BF)
-        got = swap(field.reshape((devices, slots, lats, 2 * chan_width)))
-        return (
-            got.reshape(devices, slots, lats, 2, chan_width)
-            .transpose(2, 0, 1, 3, 4)
-            .reshape(lats, devices * slots * 2, chan_width)
-        )
-
-    return forward, backward
+        got = swap(part.reshape(devices, rows, channels))
+        field = stage(behind_kernel, parted(got), table, spot, gains, weights, chan_width)
+        return swap(field).reshape(devices * rows, chan_width)
+
+    wave = jnp.arange(devices * slots * 2, dtype=jnp.int32)
+    base = wave // (2 * slots) * rows + wave % (2 * slots)
+    spots = base[None, :] + 2 * slots * jnp.arange(lats, dtype=jnp.int32)[:, None]
+    lines_all = jnp.arange(devices * rows, dtype=jnp.int32)
+    place = (lines_all[:, None] == spots.reshape(1, -1)).astype(BF)
+    base = jnp.broadcast_to(base[:, None], (base.shape[0], 128))
+    return forward, backward, base, place, 2 * slots
 
 
 def shard_paths(legendre, spec_gain, weights, lats, chan_width):
     chans = lax.axis_size("chan")
     table = lax.all_gather(legendre, "chan", axis=1, tiled=True)
-    slots = table.shape[0]
-    channels = weights.shape[1]
 
     def to_orders(values):
         return lax.all_to_all(values, "space", split_axis=1, concat_axis=0, tiled=True)
@@ -230,7 +341,8 @@
         imag = products[:, :, 1, 0] - products[:, :, 0, 1]
         return synthesis(jnp.stack([real, imag], axis=2))
 
-    return forward, backward
+    nothing = jnp.zeros((8, 128), jnp.int32)
+    return forward, backward, nothing, nothing.astype(BF), 0
 
 
 def shards(
@@ -250,10 +362,16 @@
     lon_width = lon_count // chans
     table = transform_table(order_table, lon_count)
     paths = spread_paths if legendre.shape[0] % chans == 0 else shard_paths
-    forward, backward = paths(legendre, spec_gain, spectral_weight, lats, chan_width)
-
-    point_state = chan_swap(state, 2, 1)
-    first, second = chan_rows(mlp_in, True), chan_rows(mlp_out, True)
+    forward, backward, base, place, regroup = paths(
+        legendre, spec_gain, spectral_weight, lats, chan_width
+    )
+
+    if chans == 2:
+        point_state = chan_swap_early(state, 2, 1, lats // 3)
+    else:
+        point_state = chan_swap(state, 2, 1)
+    first = chan_rows(mlp_in, True)
+    second = chan_rows(mlp_out, True)
     weighting = jnp.repeat(jnp.where(order_table == 0, 1.0, 2.0), 2).astype(BF)
     own_table = lax.dynamic_slice_in_dim(table, me * lon_width, lon_width, 0)
     inverse = (own_table * weighting[None, :]).T
@@ -261,12 +379,15 @@
     spectral = einsum("tcn,nj->tjc", state, table)
     spectral = (spectral * quad_weight[:, None, None]).astype(BF)
     synth = forward(spectral)
-    output, point_grad, part = mlp(point_state, cotangent, synth, inverse, first, second)
+    output, point_grad, part = mlp(
+        point_state, cotangent, synth, inverse, base, place, regroup, first, second
+    )
     hidden_grad = chan_swap(point_grad, 1, 2)
     field = backward(part)
+    if regroup:
+        return output, last(quad_weight, hidden_grad, field, table.T, base, regroup)
     field_grad = einsum("tjc,nj->tcn", field, table) * quad_weight[:, None, None]
-    state_grad = (hidden_grad.astype(F32) + field_grad).astype(BF)
-    return output, state_grad
+    return output, (hidden_grad.astype(F32) + field_grad).astype(BF)
 
 
 def solution(mesh):

time: 257 us -> 185 us (0.72)
  waiting for transfers between devices: 98.6 us -> 51.5 us
  local copies, waits for them, and re-layouts: 82.6 us -> 46.3 us
  Pallas kernels: 18.8 us -> 40.2 us
  matrix products: 18.4 us -> 6.12 us
  other arithmetic: 7.86 us -> 11.7 us
    ppermute x3, waiting for transfers between devices: 40.3 us -> 0.01 us  [chan_rows(): piece = lax.ppermute(mine, 'chan', ring)]
    reshape x16 -> x0, local copies, waits for them, and re-layouts: 26.9 us -> none  [the longest x1 4.81 us: forward(): got.reshape(devices, slots, lats, 2, channels).transpose(2, 0, 1, 3, 4)]
    all_to_all x4, waiting for transfers between devices: 55 us -> 33.2 us  [swap(): return lax.all_to_all(flat, BOTH, 0, 0, tiled=True)]
    pallas_call x1 -> x4, Pallas kernels: 18.8 us -> 40.2 us  [the longest x1 25.6 us: mlp(): pl.pallas_call(functools.partial(mlp_kernel, regroup), grid=(lats,), in_s...]
    dot_general x7 -> x1, matrix products: 18.4 us -> 6.12 us  [einsum(): return jnp.einsum(form, *values, preferred_element_type=F32)]
    ppermute x0 -> x2, waiting for transfers between devices: none -> 9.38 us  [chan_swap_early(): piece = lax.ppermute(piece, 'chan', [(0, 1), (1, 0)])]
    transpose x3 -> x0, local copies, waits for them, and re-layouts: 6.82 us -> none  [the longest x1 3.12 us: forward(): return got.reshape(devices, slots, lats, 2, channels).transpose(2, 0, 1,...]
    ppermute x3 -> x2, waiting for transfers between devices: 3.27 us -> 8.9 us  [chan_swap(): piece = lax.ppermute(piece, 'chan', ring)]
  transfers between devices with their start and end apart: 12 -> 13, of which waited for: 6 -> 6; matrix products, arithmetic and copies ran while one was open for 22% -> 31% of each run, Pallas kernels for 0% -> 4%
where the time goes in v1:
time: 185 us; the launch traced here: 184 us
  waiting for transfers between devices  51.5 us (28%)
  local copies, waits for them, and re-layouts  46.3 us (25%)
  Pallas kernels  40.2 us (22%)
  starting transfers between devices  27.3 us (15%)
  other arithmetic  11.7 us (6%)
  matrix products  6.12 us (3%)
    all_to_all x4, waiting for transfers between devices, swap(): return lax.all_to_all(flat, BOTH, 0, 0, tiled=True)  33.2 us
    pallas_call x1, Pallas kernels, mlp(): pl.pallas_call(functools.partial(mlp_kernel, regroup), grid=(lats,), in_s...  25.6 us
    all_to_all x4, starting transfers between devices, swap(): return lax.all_to_all(flat, BOTH, 0, 0, tiled=True)  18.9 us
    dynamic_update_slice x4, local copies, waits for them, and re-layouts, chan_rows(): lax.dynamic_update_slice_in_dim(result, other, source * rows + (1 - parit...  9.64 us
    ppermute x2, waiting for transfers between devices, chan_swap_early(): piece = lax.ppermute(piece, 'chan', [(0, 1), (1, 0)])  9.38 us
    ppermute x2, waiting for transfers between devices, chan_swap(): piece = lax.ppermute(piece, 'chan', ring)  8.9 us
    convert_element_type x2, other arithmetic, transform_table(): return (waves * (1.0 / math.sqrt(lon_count))).astype(BF)  8.04 us
    pallas_call x1, Pallas kernels, last(): pl.pallas_call(functools.partial(last_kernel, regroup), grid=(lats,), in_...  7.55 us
  transfers between devices with their start and end apart: 13, of which 6 were waited for; matrix products, arithmetic and copies ran while one was open for 31% of the time, Pallas kernels for 4%

profile of v1, /device:TPU:1, one launch (start us, length us, event | category | flops | bytes accessed | tf_op | source)
XLA Modules:
  0.0 184.1 jit_solution(4618393747958576780)
XLA Ops:
  0.6 1.2 copy.30
  1.9 0.9 constant_dynamic-slice_fusion.1
  2.7 2.1 %collective-permute-start.6 = (bf16[192,512]{0,1:T(8,128)(2,1)}, bf16[192,512]{0,1:T(8,128)(2,1)}, u32[]{:S(2)}, u32[]{:S(2)}) collective-permute-start(bf16[192,512]{0,1:T(8,128)(2,1)} %constant_dynamic-slice_fusion.1), channel_id=1, source_target_pairs={{0,1},{1,0},{2,3},{3,2},{4,5},{5,4},{6,7},{7,6},{8,9},{9,8},{10,11... | collective-permute-start | bytes 589832 | tf_op jit(solution)/shard_map/ppermute | solution.py:81
  4.8 0.8 constant_dynamic-slice_fusion.3
  5.7 1.5 collective-permute-start.3
  7.2 0.7 broadcast_in_dim.54
  7.9 0.1 mul.173
  8.0 6.1 %fusion.2 = bf16[6,192,256]{2,1,0:T(8,128)(2,1)S(1)} fusion(bf16[6,256,1024]{2,1,0:T(8,128)(2,1)} %param.9, f32[6]{0:T(128)} %quad.1, s32[192]{0:T(256)S(1)} %mul.173, s32[192]{0:T(256)S(1)} %get-tuple-element.12, s32[192]{0:T(256)S(1)} %get-tuple-element.13, pred[192]{0:T(512)(128)(4,1)S(1)} %compare_and_fusion), kind=kOutput, calls=%fused_computation.6 | convolution fusion | flops 608501760 | bytes 3738072 | tf_op jit(solution)/shard_map/tcn,nj->tjc/dot_general | solution.py:255
  14.2 0.2 reshape.118
  14.5 0.3 copy.34
  14.9 0.9 pad.4.clone
  15.8 6.1 %all-to-all-start = ((bf16[32,40,256]{2,1,0:T(8,128)(2,1)}), bf16[32,40,256]{2,1,0:T(8,128)(2,1)S(1)}, u32[]{:S(2)}, u32[]{:S(2)}) async-start(bf16[32,40,256]{2,1,0:T(8,128)(2,1)} %pad.4.clone), calls=%async_computation | async-start | bytes 1310720 | tf_op jit(solution)/shard_map/all_to_all | solution.py:273
  21.9 0.2 copy.28
  22.1 0.7 constant_dynamic-slice_fusion.2
  22.8 1.4 collective-permute-start.4
  24.2 0.8 constant_dynamic-slice_fusion.5
  25.1 3.2 %slice.7 = bf16[4,256,1024]{2,1,0:T(8,128)(2,1)} slice(bf16[6,256,1024]{2,1,0:T(8,128)(2,1)} %param.9), slice={[2:6], [0:256], [0:1024]} | slice | bytes 4194304 | tf_op jit(solution)/shard_map/slice | solution.py:58
  28.4 0.9 constant_dynamic-update-slice_fusion.5
  29.3 2.3 %constant_dynamic-slice_fusion.4 = bf16[4,256,512]{2,1,0:T(8,128)(2,1)} fusion(bf16[4,256,1024]{2,1,0:T(8,128)(2,1)} %slice.7, s32[]{:T(128)S(6)} %select_n.189), kind=kLoop, calls=%fused_computation.44 | loop fusion | bytes 2097156 | tf_op jit(solution)/shard_map/dynamic_slice | solution.py:59
  31.5 3.7 %multiply_convert_fusion.1 = bf16[1024,192]{0,1:T(8,128)(2,1)S(1)} fusion(s32[192]{0:T(256)S(1)} %mul.173, s32[192]{0:T(256)S(1)} %get-tuple-element.12, s32[192]{0:T(256)S(1)} %get-tuple-element.13, pred[192]{0:T(512)(128)(4,1)S(1)} %copy-done.13), kind=kLoop, calls=%fused_computation.23 | loop fusion | flops 3932160 | bytes 395712 | tf_op jit(solution)/shard_map/convert_element_type | solution.py:24
  35.3 1.4 collective-permute-start.1
  36.7 0.9 constant_dynamic-update-slice_fusion.4.gain
  37.6 2.8 %all-to-all-done = bf16[32,40,256]{2,1,0:T(8,128)(2,1)S(1)} async-done(((bf16[32,40,256]{2,1,0:T(8,128)(2,1)}), bf16[32,40,256]{2,1,0:T(8,128)(2,1)S(1)}, u32[]{:S(2)}, u32[]{:S(2)}) %all-to-all-start) | async-done | bytes 655392 | tf_op jit(solution)/shard_map/all_to_all | solution.py:273
  40.4 3.1 %shard_map.104 = bf16[16,2,40,512]{3,2,1,0:T(8,128)(2,1)} custom-call(bf16[16,2,40,256]{3,2,1,0:T(8,128)(2,1)S(1)} %bitcast.19, bf16[3,96,96]{2,1,0:T(8,128)(2,1)S(1)} %constant_dynamic-update-slice_fusion.6.table, s32[96,128]{1,0:T(8,128)S(1)} %broadcast_in_dim.56.base, f32[96,512]{1,0:T(8,128)S(1)} %constant_dynamic-update-slice_fusion.4.gain, ...), custom_call_target="tpu_custom_call" | custom-call | tf_op jit(solution)/shard_map/pallas_call | solution.py:247
  43.5 3.5 %all-to-all-start.1 = ((bf16[32,40,512]{2,1,0:T(8,128)(2,1)}), bf16[32,40,512]{2,1,0:T(8,128)(2,1)}, u32[]{:S(2)}, u32[]{:S(2)}) async-start(bf16[32,40,512]{2,1,0:T(8,128)(2,1)} %bitcast.5), calls=%async_computation.1 | async-start | bytes 2621440 | tf_op jit(solution)/shard_map/all_to_all | solution.py:273
  47.1 2.8 %fusion.place = bf16[1280,1152]{1,0:T(8,128)(2,1)} fusion(s32[1152]{0:T(1024)S(1)} %add.244), kind=kLoop, calls=%fused_computation.1 | loop fusion | flops 2949120 | bytes 2953728 | tf_op jit(solution)/shard_map/convert_element_type | solution.py:295
  50.0 0.2 convert_element_type.39
  50.2 0.8 multiply_bitcast_fusion.table
  51.0 0.9 broadcast_in_dim.62
  51.9 0.8 constant_dynamic-update-slice_fusion.3
  52.7 0.3 broadcast_in_dim.53
  53.0 1.6 dynamic-slice_dynamic-update-slice_fusion.1
  54.7 0.4 collective-permute-start.5
  55.2 0.9 broadcast_in_dim.63
  56.1 0.8 constant_dynamic-update-slice_fusion
  56.9 3.2 %dynamic_update_slice.56 = bf16[768,512]{0,1:T(8,128)(2,1)} dynamic-update-slice(bf16[768,512]{0,1:T(8,128)(2,1)} %constant_dynamic-update-slice_fusion, bf16[192,512]{0,1:T(8,128)(2,1)} %collective-permute-done.6, s32[]{:T(128)S(6)} %select_n.213, s32[]{:T(128)} %constant.126.clone.1) | dynamic-update-slice | bytes 393220 | tf_op jit(solution)/shard_map/dynamic_update_slice | solution.py:84
  60.1 1.6 constant_dynamic-update-slice_fusion.2
  61.8 3.4 %dynamic_update_slice.57 = bf16[768,512]{0,1:T(8,128)(2,1)} dynamic-update-slice(bf16[768,512]{0,1:T(8,128)(2,1)} %dynamic_update_slice.56, bf16[192,512]{0,1:T(8,128)(2,1)} %collective-permute-done.7, s32[]{:T(128)S(6)} %select_n.214, s32[]{:T(128)} %constant.126.clone.1) | dynamic-update-slice | bytes 393220 | tf_op jit(solution)/shard_map/dynamic_update_slice | solution.py:87
  65.2 2.3 %copy.33.second = bf16[768,512]{1,0:T(8,128)(2,1)} copy(bf16[768,512]{0,1:T(8,128)(2,1)} %dynamic_update_slice.57) | data formatting | bytes 1572864 | tf_op jit(solution)/shard_map/dynamic_update_slice | solution.py:87
  67.5 1.6 constant_dynamic-update-slice_fusion.1
  69.1 2.3 %copy.32.first = bf16[512,768]{1,0:T(8,128)(2,1)} copy(bf16[512,768]{0,1:T(8,128)(2,1)} %constant_dynamic-update-slice_fusion.1) | data formatting | bytes 1572864 | tf_op jit(solution)/shard_map/dynamic_update_slice | solution.py:87
  71.4 1.1 constant_dynamic-update-slice_fusion.8
  72.5 9.4 %collective-permute-done.1 = bf16[4,256,512]{2,1,0:T(8,128)(2,1)} collective-permute-done((bf16[4,256,512]{2,1,0:T(8,128)(2,1)}, bf16[4,256,512]{2,1,0:T(8,128)(2,1)}, u32[]{:S(2)}, u32[]{:S(2)}) %collective-permute-start.1) | collective-permute-done | bytes 1048608 | tf_op jit(solution)/shard_map/ppermute | solution.py:60
  81.9 1.3 constant_dynamic-update-slice_fusion.7.state
  83.2 0.4 all-to-all-done.1
  83.6 1.1 broadcast_in_dim.61.base
  84.8 0.1 copy-done.6
  84.9 25.6 %shard_map.105 = (bf16[6,512,512]{2,1,0:T(8,128)(2,1)}, bf16[6,512,512]{2,1,0:T(8,128)(2,1)}, bf16[1280,512]{1,0:T(8,128)(2,1)}) custom-call(bf16[6,512,512]{2,1,0:T(8,128)(2,1)} %copy-done.6, bf16[6,512,512]{2,1,0:T(8,128)(2,1)} %cot.1, bf16[1280,512]{1,0:T(8,128)(2,1)} %bitcast.6.synth, bf16[192,512]{1,0:T(8,128)(2,1)} %multiply_bitcast_fusion.table, ...), custom_call_target="tpu_custom_call" | custom-call | tf_op jit(solution)/shard_map/pallas_call | solution.py:154
  110.6 5.0 %all-to-all-start.2 = ((bf16[32,40,512]{2,1,0:T(8,128)(2,1)}), bf16[32,40,512]{2,1,0:T(8,128)(2,1)}, u32[]{:S(2)}, u32[]{:S(2)}) async-start(bf16[32,40,512]{2,1,0:T(8,128)(2,1)} %bitcast.23), calls=%async_computation.2 | async-start | bytes 2621440 | tf_op jit(solution)/shard_map/all_to_all | solution.py:273
  115.6 0.4 broadcast_in_dim.64
  115.9 1.5 copy-done.7
  117.4 1.5 constant_dynamic-slice_fusion
  118.9 1.4 collective-permute-start.8
  120.3 26.5 %all-to-all-done.2 = bf16[32,40,512]{2,1,0:T(8,128)(2,1)} async-done(((bf16[32,40,512]{2,1,0:T(8,128)(2,1)}), bf16[32,40,512]{2,1,0:T(8,128)(2,1)}, u32[]{:S(2)}, u32[]{:S(2)}) %all-to-all-start.2) | async-done | bytes 1310752 | tf_op jit(solution)/shard_map/all_to_all | solution.py:273
  146.7 1.2 copy-done.1
  148.0 3.9 %shard_map.106 = bf16[16,2,40,256]{3,2,1,0:T(8,128)(2,1)S(1)} custom-call(bf16[16,2,40,512]{3,2,1,0:T(8,128)(2,1)} %bitcast.11.got, bf16[3,96,96]{2,1,0:T(8,128)(2,1)S(1)} %constant_dynamic-update-slice_fusion.6.table, s32[96,128]{1,0:T(8,128)S(1)} %broadcast_in_dim.56.base, f32[96,512]{1,0:T(8,128)S(1)} %constant_dynamic-update-slice_fusion.4.gain, ...), custom_call_target="tpu_custom_call" | custom-call | tf_op jit(solution)/shard_map/pallas_call | solution.py:247
  151.8 0.8 copy-done.2
  152.7 4.3 %all-to-all-start.3 = ((bf16[32,40,256]{2,1,0:T(8,128)(2,1)}), bf16[32,40,256]{2,1,0:T(8,128)(2,1)}, u32[]{:S(2)}, u32[]{:S(2)}) async-start(bf16[32,40,256]{2,1,0:T(8,128)(2,1)} %bitcast.20), calls=%async_computation.3 | async-start | bytes 1310720 | tf_op jit(solution)/shard_map/all_to_all | solution.py:273
  157.0 4.3 %multiply_convert_fusion.table = bf16[192,1024]{1,0:T(8,128)(2,1)} fusion(s32[192]{0:T(256)S(1)} %mul.173, s32[192]{0:T(256)S(1)} %get-tuple-element.12, s32[192]{0:T(256)S(1)} %get-tuple-element.13, pred[192]{0:T(512)(128)(4,1)S(1)} %copy-done.14), kind=kLoop, calls=%fused_computation.19 | loop fusion | flops 3932160 | bytes 395712 | tf_op jit(solution)/shard_map/convert_element_type | solution.py:24
  161.4 8.9 %collective-permute-done.8 = bf16[6,256,512]{2,1,0:T(8,128)(2,1)} collective-permute-done((bf16[6,256,512]{2,1,0:T(8,128)(2,1)}, bf16[6,256,512]{2,1,0:T(8,128)(2,1)}, u32[]{:S(2)}, u32[]{:S(2)}) %collective-permute-start.8) | collective-permute-done | bytes 1572896 | tf_op jit(solution)/shard_map/ppermute | solution.py:40
  170.3 1.7 constant_dynamic-update-slice_fusion.9.hidden_grad
  171.9 3.6 %all-to-all-done.3 = bf16[32,40,256]{2,1,0:T(8,128)(2,1)} async-done(((bf16[32,40,256]{2,1,0:T(8,128)(2,1)}), bf16[32,40,256]{2,1,0:T(8,128)(2,1)}, u32[]{:S(2)}, u32[]{:S(2)}) %all-to-all-start.3) | async-done | bytes 655392 | tf_op jit(solution)/shard_map/all_to_all | solution.py:273
  175.5 1.0 copy-done.4
  176.5 7.6 %shard_map.107 = bf16[6,256,1024]{2,1,0:T(8,128)(2,1)} custom-call(f32[6]{0:T(128)S(1)} %copy-done.5, bf16[6,256,1024]{2,1,0:T(8,128)(2,1)S(1)} %constant_dynamic-update-slice_fusion.9.hidden_grad, bf16[1280,256]{1,0:T(8,128)(2,1)} %bitcast.13.field, bf16[192,1024]{1,0:T(8,128)(2,1)S(1)} %copy-done.4, s32[192,128]{1,0:T(8,128)S(1)} %copy-done.3), custom_call_target="tpu_custom_call" | custom-call | tf_op jit(solution)/shard_map/pallas_call | solution.py:180
  (51 shorter events, 0.9 us)
Async XLA Ops:
  1.9 6.2 %copy-start.8 = (bf16[384,512]{0,1:T(8,128)(2,1)}, bf16[384,512]{0,1:T(8,128)(2,1)S(1)}, u32[]{:S(2)}) copy-start(bf16[384,512]{0,1:T(8,128)(2,1)S(1)} %copy.30) | copy-start | bytes 1179652
  2.7 51.8 %collective-permute-start.6 = (bf16[192,512]{0,1:T(8,128)(2,1)}, bf16[192,512]{0,1:T(8,128)(2,1)}, u32[]{:S(2)}, u32[]{:S(2)}) collective-permute-start(bf16[192,512]{0,1:T(8,128)(2,1)} %constant_dynamic-slice_fusion.1), channel_id=1, source_target_pairs={{0,1},{1,0},{2,3},{3,2},{4,5},{5,4},{6,7},{7,6},{8,9},{9,8},{10,11... | collective-permute-start | bytes 589832 | tf_op jit(solution)/shard_map/ppermute | solution.py:81
  5.6 29.6 %collective-permute-start.2 = (bf16[3,48,96]{2,1,0:T(8,128)(2,1)S(1)}, bf16[3,48,96]{2,1,0:T(8,128)(2,1)S(1)}, u32[]{:S(2)}, u32[]{:S(2)}) collective-permute-start(bf16[3,48,96]{2,1,0:T(8,128)(2,1)S(1)} %get-tuple-element.10), channel_id=1, source_target_pairs={{0,1},{1,0},{2,3},{3,2},{4,5},{5,4},{6,7},{7,6},{8,9},{9,8},{10,11... | collective-permute-start | bytes 82952 | tf_op jit(solution)/shard_map/ppermute | solution.py:40
  5.7 31.0 %collective-permute-start.3 = (f32[48,512]{1,0:T(8,128)}, f32[48,512]{1,0:T(8,128)}, u32[]{:S(2)}, u32[]{:S(2)}) collective-permute-start(f32[48,512]{1,0:T(8,128)} %param.14), channel_id=1, source_target_pairs={{0,1},{1,0},{2,3},{3,2},{4,5},{5,4},{6,7},{7,6},{8,9},{9,8},{10,11... | collective-permute-start | bytes 294920 | tf_op jit(solution)/shard_map/ppermute | solution.py:81
  7.2 7.0 %copy-start.12 = (pred[192]{0:T(512)(128)(4,1)}, pred[192]{0:T(512)(128)(4,1)S(1)}, u32[]{:S(2)}) copy-start(pred[192]{0:T(512)(128)(4,1)S(1)} %compare_and_fusion) | copy-start | bytes 580
  14.2 7.8 %copy-start.10 = (bf16[256,768]{1,0:T(8,128)(2,1)S(1)}, bf16[256,768]{1,0:T(8,128)(2,1)}, u32[]{:S(2)}) copy-start(bf16[256,768]{1,0:T(8,128)(2,1)} %param.16) | copy-start | bytes 1179652
  14.9 9.3 %slice-start = ((bf16[6,256,1024]{2,1,0:T(8,128)(2,1)}), bf16[2,256,1024]{2,1,0:T(8,128)(2,1)S(1)}, s32[]{:S(2)}) async-start(bf16[6,256,1024]{2,1,0:T(8,128)(2,1)} %param.9), calls=%async_computation.4 | async-start | bytes 2097152 | tf_op jit(solution)/shard_map/slice | solution.py:58
  15.8 24.6 %all-to-all-start = ((bf16[32,40,256]{2,1,0:T(8,128)(2,1)}), bf16[32,40,256]{2,1,0:T(8,128)(2,1)S(1)}, u32[]{:S(2)}, u32[]{:S(2)}) async-start(bf16[32,40,256]{2,1,0:T(8,128)(2,1)} %pad.4.clone), calls=%async_computation | async-start | bytes 1310720 | tf_op jit(solution)/shard_map/all_to_all | solution.py:273
  22.8 31.9 %collective-permute-start.4 = (bf16[128,768]{0,1:T(8,128)(2,1)}, bf16[128,768]{0,1:T(8,128)(2,1)}, u32[]{:S(2)}, u32[]{:S(2)}) collective-permute-start(bf16[128,768]{0,1:T(8,128)(2,1)} %constant_dynamic-slice_fusion.2), channel_id=1, source_target_pairs={{0,1},{1,0},{2,3},{3,2},{4,5},{5,4},{6,7},{7,6},{8,9},{9,8},{10,11... | collective-permute-start | bytes 589832 | tf_op jit(solution)/shard_map/ppermute | solution.py:81
  25.0 46.4 %collective-permute-start = (bf16[2,256,512]{2,1,0:T(8,128)(2,1)}, bf16[2,256,512]{2,1,0:T(8,128)(2,1)}, u32[]{:S(2)}, u32[]{:S(2)}) collective-permute-start(bf16[2,256,512]{2,1,0:T(8,128)(2,1)} %constant_dynamic-slice_fusion.5), channel_id=1, source_target_pairs={{0,1},{1,0},{2,3},{3,2},{4,5},{5,4},{6,7},{7,6},{8,9},{9,8},{10,11... | collective-permute-start | bytes 1572872 | tf_op jit(solution)/shard_map/ppermute | solution.py:60
  25.1 6.4 %copy-start.13 = (pred[192]{0:T(512)(128)(4,1)S(1)}, pred[192]{0:T(512)(128)(4,1)}, u32[]{:S(2)}) copy-start(pred[192]{0:T(512)(128)(4,1)} %copy-done.12) | copy-start | bytes 580
  25.1 15.3 %copy-start = (bf16[2,512,512]{2,1,0:T(8,128)(2,1)S(1)}, bf16[2,512,512]{2,1,0:T(8,128)(2,1)}, u32[]{:S(2)}) copy-start(bf16[2,512,512]{2,1,0:T(8,128)(2,1)} %weights.3) | copy-start | bytes 3145732
  35.3 46.6 %collective-permute-start.1 = (bf16[4,256,512]{2,1,0:T(8,128)(2,1)}, bf16[4,256,512]{2,1,0:T(8,128)(2,1)}, u32[]{:S(2)}, u32[]{:S(2)}) collective-permute-start(bf16[4,256,512]{2,1,0:T(8,128)(2,1)} %constant_dynamic-slice_fusion.4), channel_id=1, source_target_pairs={{0,1},{1,0},{2,3},{3,2},{4,5},{5,4},{6,7},{7,6},{8,9},{9,8},{10,11... | collective-permute-start | bytes 3145736 | tf_op jit(solution)/shard_map/ppermute | solution.py:60
  43.5 6.4 %copy-start.11 = (s32[96]{0:T(128)S(1)}, s32[96]{0:T(128)}, u32[]{:S(2)}) copy-start(s32[96]{0:T(128)} %param.11) | copy-start | bytes 1156
  43.5 40.1 %all-to-all-start.1 = ((bf16[32,40,512]{2,1,0:T(8,128)(2,1)}), bf16[32,40,512]{2,1,0:T(8,128)(2,1)}, u32[]{:S(2)}, u32[]{:S(2)}) async-start(bf16[32,40,512]{2,1,0:T(8,128)(2,1)} %bitcast.5), calls=%async_computation.1 | async-start | bytes 2621440 | tf_op jit(solution)/shard_map/all_to_all | solution.py:273
  52.7 3.4 %copy-start.9 = (bf16[384,512]{0,1:T(8,128)(2,1)S(1)}, bf16[384,512]{0,1:T(8,128)(2,1)}, u32[]{:S(2)}) copy-start(bf16[384,512]{0,1:T(8,128)(2,1)} %copy-done.8) | copy-start | bytes 1179652
  54.6 7.2 %collective-permute-start.7 = (bf16[192,512]{0,1:T(8,128)(2,1)}, bf16[192,512]{0,1:T(8,128)(2,1)}, u32[]{:S(2)}, u32[]{:S(2)}) collective-permute-start(bf16[192,512]{0,1:T(8,128)(2,1)} %collective-permute-done.6), channel_id=1, source_target_pairs={{0,2},{2,0},{4,6},{6,4},{8,10},{10,8},{12,14},{14,12},{16,18},{18,... | collective-permute-start | bytes 589832 | tf_op jit(solution)/shard_map/ppermute | solution.py:83
  54.7 12.8 %collective-permute-start.5 = (bf16[128,768]{0,1:T(8,128)(2,1)}, bf16[128,768]{0,1:T(8,128)(2,1)}, u32[]{:S(2)}, u32[]{:S(2)}) collective-permute-start(bf16[128,768]{0,1:T(8,128)(2,1)} %collective-permute-done.4), channel_id=1, source_target_pairs={{0,2},{2,0},{4,6},{6,4},{8,10},{10,8},{12,14},{14,12},{16,18},{18,... | collective-permute-start | bytes 589832 | tf_op jit(solution)/shard_map/ppermute | solution.py:83
  83.2 1.7 copy-start.6
  110.6 36.2 %all-to-all-start.2 = ((bf16[32,40,512]{2,1,0:T(8,128)(2,1)}), bf16[32,40,512]{2,1,0:T(8,128)(2,1)}, u32[]{:S(2)}, u32[]{:S(2)}) async-start(bf16[32,40,512]{2,1,0:T(8,128)(2,1)} %bitcast.23), calls=%async_computation.2 | async-start | bytes 2621440 | tf_op jit(solution)/shard_map/all_to_all | solution.py:273
  115.5 1.9 %copy-start.7 = (bf16[6,512,512]{2,1,0:T(8,128)(2,1)S(1)}, bf16[6,512,512]{2,1,0:T(8,128)(2,1)}, u32[]{:S(2)}) copy-start(bf16[6,512,512]{2,1,0:T(8,128)(2,1)} %get-tuple-element.6) | copy-start | bytes 9437188
  118.9 38.1 %copy-start.14 = (pred[192]{0:T(512)(128)(4,1)S(1)}, pred[192]{0:T(512)(128)(4,1)}, u32[]{:S(2)}) copy-start(pred[192]{0:T(512)(128)(4,1)} %copy-done.12) | copy-start | bytes 580
  118.9 51.4 %collective-permute-start.8 = (bf16[6,256,512]{2,1,0:T(8,128)(2,1)}, bf16[6,256,512]{2,1,0:T(8,128)(2,1)}, u32[]{:S(2)}, u32[]{:S(2)}) collective-permute-start(bf16[6,256,512]{2,1,0:T(8,128)(2,1)} %get-tuple-element.8), channel_id=1, source_target_pairs={{0,1},{1,0},{2,3},{3,2},{4,5},{5,4},{6,7},{7,6},{8,9},{9,8},{10,11... | collective-permute-start | bytes 4718600 | tf_op jit(solution)/shard_map/ppermute | solution.py:40
  146.7 1.2 copy-start.1
  151.8 0.8 copy-start.2
  152.7 22.8 %copy-start.3 = (s32[192,128]{1,0:T(8,128)S(1)}, s32[192,128]{1,0:T(8,128)}, u32[]{:S(2)}) copy-start(s32[192,128]{1,0:T(8,128)} %broadcast_in_dim.61.base) | copy-start | bytes 294916
  152.7 22.8 %copy-start.5 = (f32[6]{0:T(128)S(1)}, f32[6]{0:T(128)}, u32[]{:S(2)}) copy-start(f32[6]{0:T(128)} %quad.1) | copy-start | bytes 76
  152.7 22.8 %all-to-all-start.3 = ((bf16[32,40,256]{2,1,0:T(8,128)(2,1)}), bf16[32,40,256]{2,1,0:T(8,128)(2,1)}, u32[]{:S(2)}, u32[]{:S(2)}) async-start(bf16[32,40,256]{2,1,0:T(8,128)(2,1)} %bitcast.20), calls=%async_computation.3 | async-start | bytes 1310720 | tf_op jit(solution)/shard_map/all_to_all | solution.py:273
  175.5 1.0 copy-start.4
